TPU v7x, 32 devices: a whole 2x2x4 slice. The times are simulated.
32 devices in a mesh: grp: 2 (over y), ctx: 4 (over z), head: 2 (over x), rep: 2 (over core).
Axes of the slice: x: 2, y: 2, z: 4, core: 2. Of those that a mesh axis runs over, the one named last changes fastest.
Arguments:
- queries: bfloat16 [8192, 2048], P(('grp', 'ctx', 'head', 'rep')), parts along dimension 0, may hold values from -10 to 10
- keys: bfloat16 [8192, 2048], P(('grp', 'ctx', 'head', 'rep')), parts along dimension 0, may hold values from -10 to 10
- values: bfloat16 [8192, 2048], P(('grp', 'ctx', 'head', 'rep')), parts along dimension 0, may hold values from -6 to 6
- reads: int32 [16, 8], P('grp'), parts along dimension 0, may hold values from 0 to 1, as said below
- owner: int32 [16], P('grp'), parts along dimension 0, may hold values from 0 to 7, as said below
Outputs:
- attended: bfloat16 [8192, 2048], P(('grp', 'ctx', 'head', 'rep')), parts along dimension 0
There are 2 independent parts, one for each index of `grp`. A program takes and returns all parts, laid end to end along the dimension named above; each array names one. Nothing has to cross between parts.
Inputs may be any that keep to these rules, and one draw needn't show every extreme that they name: `owner`: A permutation of the blocks in which sequence block b sits in slot b or in slot b with its lowest bit flipped. Every block reads itself; reads[kb, qb] is nonzero only where |kb - qb| <= 2 and |owner[kb] - owner[qb]| <= 3.
All inputs are finite; a program needn't handle non-finite values.
Results may differ from a plain program's by a relative error of at most 0.0047.
Values may be sent and summed in bfloat16 or wider, within the bound.
No kernel may reach another device: no remote copies, remote signals or barrier semaphores. Data moves between devices by JAX's collectives and lax.ppermute only.
A program may use at most 64 MiB of HBM per device.

v0:
```python
import math
import jax
import jax.numpy as jnp
from jax import lax
from jax.sharding import PartitionSpec as P

HEAD_DIM = 64
BLOCK = 512
REACH = 3


def from_behind(x, axis, by):
    devices = lax.axis_size(axis)
    pairs = [(i, i + by) for i in range(devices) if 0 <= i + by < devices]
    return lax.ppermute(x, axis, pairs)


def shards(queries, keys, values, reads, owner):
    query_heads, key_heads, value_heads = (
        lax.all_to_all(queries, ("head", "rep"), split_axis=1, concat_axis=0, tiled=True),
        lax.all_to_all(keys, ("head", "rep"), split_axis=1, concat_axis=0, tiled=True),
        lax.all_to_all(values, ("head", "rep"), split_axis=1, concat_axis=0, tiled=True),
    )
    row_count, feat_width = query_heads.shape
    heads_dev = feat_width // HEAD_DIM
    blk_dev = row_count // BLOCK
    reach_devs = -(-REACH // blk_dev)
    pair_kv = jnp.stack([key_heads, value_heads])
    lower_list = []
    upper_list = []
    moving = pair_kv
    for hop_index in range(reach_devs):
        moving = from_behind(moving, "ctx", 1)
        lower_list.insert(0, moving)
    moving = pair_kv
    for hop_index in range(reach_devs):
        moving = from_behind(moving, "ctx", -1)
        upper_list.append(moving)
    pieces = lower_list + [pair_kv] + upper_list
    window = jnp.concatenate(pieces, axis=1)
    highest = lax.Precision.HIGHEST
    block_count = reads.shape[0]
    slots = jnp.arange(block_count, dtype=jnp.int32)
    placed = (owner[:, None] == slots[None, :]).astype(jnp.float32)
    slot_reads = jnp.dot(
        jnp.dot(placed.T, reads.astype(jnp.float32), precision=highest), placed, precision=highest
    )
    padded_reads = jnp.pad(slot_reads, ((REACH, REACH), (0, 0)))
    ctx_index = lax.axis_index("ctx")
    scale_factor = 1.0 / math.sqrt(HEAD_DIM)
    tile_rows = min(512, BLOCK)
    tile_count = row_count // tile_rows

    def attend_tile(tile_id):
        local_block = tile_id * tile_rows // BLOCK
        query_slot = ctx_index * blk_dev + local_block
        column = lax.dynamic_index_in_dim(padded_reads, query_slot, 1, keepdims=False)
        allowed = lax.dynamic_slice_in_dim(column, query_slot, 2 * REACH + 1)
        query_tile = lax.dynamic_slice_in_dim(query_heads, tile_id * tile_rows, tile_rows, 0)
        query_tile = query_tile.reshape(tile_rows, heads_dev, HEAD_DIM)

        def key_block(relative):
            start = (reach_devs * blk_dev + local_block + relative) * BLOCK
            picked = lax.dynamic_slice_in_dim(window, start, BLOCK, 1)
            return picked.reshape(2, BLOCK, heads_dev, HEAD_DIM)

        def block_scores(kv_block):
            return (
                jnp.einsum(
                    "qhd,khd->hqk", query_tile, kv_block[0], preferred_element_type=jnp.float32
                )
                * scale_factor
            )

        def add_weights(pair, scores, value_block, row_max):
            weights = jnp.exp(scores - row_max[:, :, None])
            row_total = pair[1] + jnp.sum(weights, axis=-1)
            rounded = weights.astype(jnp.bfloat16)
            accum_out = pair[0] + jnp.einsum(
                "hqk,khd->qhd", rounded, value_block, preferred_element_type=jnp.float32
            )
            return (accum_out, row_total)

        row_max = jnp.full((heads_dev, tile_rows), -jnp.inf, jnp.float32)
        for position in range(2 * REACH + 1):
            is_read = allowed[position] > 0.5
            kv_block = key_block(position - REACH)
            row_max = lax.cond(
                is_read,
                lambda current, chosen=kv_block: jnp.maximum(
                    current, jnp.max(block_scores(chosen), axis=-1)
                ),
                lambda current: current,
                row_max,
            )
        totals = (
            jnp.zeros((tile_rows, heads_dev, HEAD_DIM), jnp.float32),
            jnp.zeros((heads_dev, tile_rows), jnp.float32),
        )
        for position in range(2 * REACH + 1):
            is_read = allowed[position] > 0.5
            kv_block = key_block(position - REACH)
            totals = lax.cond(
                is_read,
                lambda pair, chosen=kv_block: add_weights(
                    pair, block_scores(chosen), chosen[1], row_max
                ),
                lambda pair: pair,
                totals,
            )
        result = totals[0] / jnp.transpose(totals[1])[:, :, None]
        return result.reshape(tile_rows, feat_width).astype(jnp.bfloat16)

    tiles_out = lax.map(attend_tile, jnp.arange(tile_count, dtype=jnp.int32))
    attended = tiles_out.reshape(row_count, feat_width)
    return lax.all_to_all(attended, ("head", "rep"), split_axis=0, concat_axis=1, tiled=True)


def solution(mesh):
    placed = (
        P(("grp", "ctx", "head", "rep"), None),
        P(("grp", "ctx", "head", "rep"), None),
        P(("grp", "ctx", "head", "rep"), None),
        P("grp", None),
        P("grp"),
    )
    return jax.shard_map(
        shards,
        mesh=mesh,
        in_specs=placed,
        out_specs=P(("grp", "ctx", "head", "rep"), None),
        check_vma=False,
    )
```

profile of v0, /device:TPU:20, one launch (start us, length us, event | category | flops | bytes accessed | tf_op | source)
XLA Modules:
  0.0 273.8 jit_solution(7795582679675282533)
XLA Ops:
  0.0 2.3 copy.60
  2.3 3.5 %all-to-all-start = ((bf16[256,4,512]{0,2,1:T(8,128)(2,1)}), bf16[256,4,512]{0,2,1:T(8,128)(2,1)S(1)}, u32[]{:S(2)}, u32[]{:S(2)}) async-start(bf16[256,4,512]{0,2,1:T(8,128)(2,1)} %bitcast.46), calls=%async_computation | async-start | bytes 2097152 | tf_op jit(solution)/shard_map/all_to_all | solution.py:21
  5.8 2.3 copy.62
  8.1 12.1 %all-to-all-done = bf16[256,4,512]{0,2,1:T(8,128)(2,1)S(1)} async-done(((bf16[256,4,512]{0,2,1:T(8,128)(2,1)}), bf16[256,4,512]{0,2,1:T(8,128)(2,1)S(1)}, u32[]{:S(2)}, u32[]{:S(2)}) %all-to-all-start) | async-done | bytes 1048608 | tf_op jit(solution)/shard_map/all_to_all | solution.py:21
  20.2 3.5 %all-to-all-start.1 = ((bf16[256,4,512]{0,2,1:T(8,128)(2,1)}), bf16[256,4,512]{0,2,1:T(8,128)(2,1)S(1)}, u32[]{:S(2)}, u32[]{:S(2)}) async-start(bf16[256,4,512]{0,2,1:T(8,128)(2,1)} %bitcast.49), calls=%async_computation.1 | async-start | bytes 2097152 | tf_op jit(solution)/shard_map/all_to_all | solution.py:22
  24.3 13.8 %all-to-all-done.1 = bf16[256,4,512]{0,2,1:T(8,128)(2,1)S(1)} async-done(((bf16[256,4,512]{0,2,1:T(8,128)(2,1)}), bf16[256,4,512]{0,2,1:T(8,128)(2,1)S(1)}, u32[]{:S(2)}, u32[]{:S(2)}) %all-to-all-start.1) | async-done | bytes 1048608 | tf_op jit(solution)/shard_map/all_to_all | solution.py:22
  38.9 3.5 %collective-permute-start = (bf16[2,1024,512]{2,1,0:T(8,128)(2,1)S(1)}, bf16[2,1024,512]{2,1,0:T(8,128)(2,1)}, u32[]{:S(2)}, u32[]{:S(2)}) collective-permute-start(bf16[2,1024,512]{2,1,0:T(8,128)(2,1)S(1)} %pad_maximum_fusion), channel_id=1, source_target_pairs={{0,4},{4,8},{8,12},{1,5},{5,9},{9,13},{2,6},{6,10},{10,14},{3,7},{... | collective-permute-start | bytes 6291464 | tf_op jit(solution)/shard_map/ppermute | solution.py:15
  42.3 2.4 collective-permute-start.2
  44.7 43.2 %collective-permute-done = bf16[2,1024,512]{2,1,0:T(8,128)(2,1)} collective-permute-done((bf16[2,1024,512]{2,1,0:T(8,128)(2,1)S(1)}, bf16[2,1024,512]{2,1,0:T(8,128)(2,1)}, u32[]{:S(2)}, u32[]{:S(2)}) %collective-permute-start) | collective-permute-done | bytes 2097184 | tf_op jit(solution)/shard_map/ppermute | solution.py:15
  87.9 3.5 %collective-permute-start.1 = (bf16[2,1024,512]{2,1,0:T(8,128)(2,1)}, bf16[2,1024,512]{2,1,0:T(8,128)(2,1)}, u32[]{:S(2)}, u32[]{:S(2)}) collective-permute-start(bf16[2,1024,512]{2,1,0:T(8,128)(2,1)} %collective-permute-done), channel_id=1, source_target_pairs={{0,4},{4,8},{8,12},{1,5},{5,9},{9,13},{2,6},{6,10},{10,14},{3,7},{... | collective-permute-start | bytes 6291464 | tf_op jit(solution)/shard_map/ppermute | solution.py:15
  91.4 2.4 collective-permute-start.3
  93.8 2.3 copy.64
  96.1 3.5 %all-to-all-start.2 = ((bf16[256,4,512]{0,2,1:T(8,128)(2,1)}), bf16[256,4,512]{0,2,1:T(8,128)(2,1)S(1)}, u32[]{:S(2)}, u32[]{:S(2)}) async-start(bf16[256,4,512]{0,2,1:T(8,128)(2,1)} %bitcast.222), calls=%async_computation.2 | async-start | bytes 2097152 | tf_op jit(solution)/shard_map/all_to_all | solution.py:20
  100.2 13.8 %all-to-all-done.2 = bf16[256,4,512]{0,2,1:T(8,128)(2,1)S(1)} async-done(((bf16[256,4,512]{0,2,1:T(8,128)(2,1)}), bf16[256,4,512]{0,2,1:T(8,128)(2,1)S(1)}, u32[]{:S(2)}, u32[]{:S(2)}) %all-to-all-start.2) | async-done | bytes 1048608 | tf_op jit(solution)/shard_map/all_to_all | solution.py:20
  115.3 21.0 %collective-permute-done.1 = bf16[2,1024,512]{2,1,0:T(8,128)(2,1)} collective-permute-done((bf16[2,1024,512]{2,1,0:T(8,128)(2,1)}, bf16[2,1024,512]{2,1,0:T(8,128)(2,1)}, u32[]{:S(2)}, u32[]{:S(2)}) %collective-permute-start.1) | collective-permute-done | bytes 2097184 | tf_op jit(solution)/shard_map/ppermute | solution.py:15
  136.3 3.1 %constant_dynamic-update-slice_fusion.5 = bf16[2,5120,512]{2,1,0:T(8,128)(2,1)} fusion(bf16[2,1024,512]{2,1,0:T(8,128)(2,1)} %collective-permute-done.1), kind=kLoop, calls=%fused_computation.133 | loop fusion | bytes 4194304
  139.4 3.1 %constant_dynamic-update-slice_fusion.4 = bf16[2,5120,512]{2,1,0:T(8,128)(2,1)} fusion(bf16[2,5120,512]{2,1,0:T(8,128)(2,1)} %constant_dynamic-update-slice_fusion.5, bf16[2,1024,512]{2,1,0:T(8,128)(2,1)} %collective-permute-done), kind=kLoop, calls=%fused_computation.132 | loop fusion | bytes 4194304
  144.0 3.0 %constant_dynamic-update-slice_fusion.2 = bf16[2,5120,512]{2,1,0:T(8,128)(2,1)} fusion(bf16[2,5120,512]{2,1,0:T(8,128)(2,1)} %constant_dynamic-update-slice_fusion.3, bf16[2,1024,512]{2,1,0:T(8,128)(2,1)} %collective-permute-done.2), kind=kLoop, calls=%fused_computation.130 | loop fusion | bytes 4194304
  147.0 3.1 %constant_dynamic-update-slice_fusion.1 = bf16[2,5120,512]{2,1,0:T(8,128)(2,1)} fusion(bf16[2,5120,512]{2,1,0:T(8,128)(2,1)} %constant_dynamic-update-slice_fusion.2, bf16[2,1024,512]{2,1,0:T(8,128)(2,1)} %collective-permute-done.3), kind=kLoop, calls=%fused_computation.129 | loop fusion | bytes 4194304 | tf_op jit(solution)/shard_map/concatenate | solution.py:40
  150.1 13.8 %copy.66 = bf16[2,5120,512]{1,2,0:T(8,128)(2,1)} copy(bf16[2,5120,512]{2,1,0:T(8,128)(2,1)} %constant_dynamic-update-slice_fusion.1) | data formatting | bytes 20971520 | tf_op jit(solution)/shard_map/while | solution.py:114
  163.9 90.1 %while.13 = (s32[]{:T(128)}, bf16[2,512,512]{2,1,0:T(8,128)(2,1)}, s32[2]{0:T(128)S(1)}, s32[]{:T(128)}, f32[14,8]{0,1:T(8,128)S(1)}, /*index=5*/bf16[2,5120,512...) while((s32[]{:T(128)}, bf16[2,512,512]{2,1,0:T(8,128)(2,1)}, ...), condition=%wide.region_43.44_spmd, body=%wide.region_0.43_spmd.sunk | while | flops 5756674048 | bytes 200296880 | solution.py:114
  165.2 5.5 %constant_dynamic-slice_fusion.10 = (bf16[2,512,512]{1,2,0:T(8,128)(2,1)S(1)}, bf16[2,512,512]{1,2,0:T(8,128)(2,1)}, bf16[2,512,512]{1,2,0:T(8,128)(2,1)}, bf16[...) fusion(bf16[2,5120,512]{1,2,0:T(8,128)(2,1)} %get-tuple-element, ...), kind=kLoop, calls=%fused_computation.120.clone.1 | loop fusion | bytes 14680092 | tf_op jit(solution)/shard_map/while/body/eval_jaxpr/dynamic_slice | solution.py:64
  174.5 2.4 conditional.29
  174.5 2.3 multiply_reduce_fusion.1
  178.0 2.4 conditional.31
  178.0 2.3 multiply_reduce_fusion.3
  181.1 2.4 conditional.32
  181.1 2.3 multiply_reduce_fusion.4
  184.1 2.4 conditional.33
  184.1 2.3 multiply_reduce_fusion.5
  188.6 4.8 %conditional.36 = ((f32[512,8,64]{0,2,1:T(8,128)S(1)}, f32[8,512]{1,0:T(8,128)S(1)})) conditional(s32[]{:T(128)} %bitcast.175, (f32[512,8,64]{0,2,1:T(8,128)S(1)}, f32[8,512]{1,0:T(8,128)S(1)}) %conditional.35, (bf16[2,512,8,64]{1,3,2,0:T(8,128)(2,1)}, bf16[512,8,64]{0,2,1:T(8,128)(2,1)S(1)}, f32[8,512]{1,0:T(8,128)S(1)}, ...), branch_computations={%region_25.25_spmd, %region_26.27_spmd} | conditional | flops 549715968 | bytes 24739892 | solution.py:103
  188.6 3.0 %fusion.29 = (f32[8,512]{1,0:T(8,128)S(1)}, f32[8,512,512]{1,2,0:T(8,128)S(1)}) fusion(f32[8,512]{1,0:T(8,128)S(1)} %get-tuple-element.344, bf16[512,8,64]{0,2,1:T(8,128)(2,1)S(1)} %get-tuple-element.342, bf16[2,512,8,64]{1,3,2,0:T(8,128)(2,1)} %get-tuple-element.343), kind=kOutput, calls=%fused_computation.35 | convolution fusion | flops 274722816 | bytes 9469952 | tf_op jit(solution)/shard_map/while/body/eval_jaxpr/cond/branch_1_fun/qhd,khd->hqk/dot_general | solution.py:69
  191.6 1.8 fusion.38
  193.5 4.8 %conditional.38 = ((f32[512,8,64]{0,2,1:T(8,128)S(1)}, f32[8,512]{1,0:T(8,128)S(1)})) conditional(s32[]{:T(128)} %bitcast.173, (f32[512,8,64]{0,2,1:T(8,128)S(1)}, f32[8,512]{1,0:T(8,128)S(1)}) %get-tuple-element.654, (bf16[2,512,8,64]{1,3,2,0:T(8,128)(2,1)}, bf16[512,8,64]{0,2,1:T(8,128)(2,1)S(1)}, f32[8,512]{1,0:T(8,128)S(1)}, ...), branch_computations={%region_31.31_spmd, %region_32.33_spmd} | conditional | flops 549715968 | bytes 24739892 | solution.py:103
  193.5 3.0 %fusion.65 = (f32[8,512]{1,0:T(8,128)S(1)}, f32[8,512,512]{1,2,0:T(8,128)S(1)}) fusion(f32[8,512]{1,0:T(8,128)S(1)} %get-tuple-element.354, bf16[512,8,64]{0,2,1:T(8,128)(2,1)S(1)} %get-tuple-element.352, bf16[2,512,8,64]{1,3,2,0:T(8,128)(2,1)} %get-tuple-element.353), kind=kOutput, calls=%fused_computation.63 | convolution fusion | flops 274722816 | bytes 9469952 | tf_op jit(solution)/shard_map/while/body/eval_jaxpr/cond/branch_1_fun/qhd,khd->hqk/dot_general | solution.py:69
  196.5 1.8 fusion.74
  198.3 3.9 %conditional.39 = ((f32[512,8,64]{0,2,1:T(8,128)S(1)}, f32[8,512]{1,0:T(8,128)S(1)})) conditional(s32[]{:T(128)} %bitcast.172, (f32[512,8,64]{0,2,1:T(8,128)S(1)}, f32[8,512]{1,0:T(8,128)S(1)}) %get-tuple-element.655, (bf16[2,512,8,64]{1,3,2,0:T(8,128)(2,1)S(1)}, bf16[512,8,64]{0,2,1:T(8,128)(2,1)S(1)}, f32[8,512]{1,0:T(8,128)S(1)}, ...), branch_computations={%region_34.34_spmd, %region_35.36_spmd} | conditional | flops 549715968 | bytes 20545560 | solution.py:103
  198.3 2.0 fusion.83
  200.4 1.8 fusion.92
  202.2 4.8 %conditional.40 = ((f32[512,8,64]{0,2,1:T(8,128)S(1)}, f32[8,512]{1,0:T(8,128)S(1)})) conditional(s32[]{:T(128)} %bitcast.171, (f32[512,8,64]{0,2,1:T(8,128)S(1)}, f32[8,512]{1,0:T(8,128)S(1)}) %get-tuple-element.656, (bf16[2,512,8,64]{1,3,2,0:T(8,128)(2,1)}, bf16[512,8,64]{0,2,1:T(8,128)(2,1)S(1)}, f32[8,512]{1,0:T(8,128)S(1)}, ...), branch_computations={%region_37.37_spmd, %region_38.39_spmd} | conditional | flops 549715968 | bytes 24739892 | solution.py:103
  202.2 3.0 %fusion.101 = (f32[8,512]{1,0:T(8,128)S(1)}, f32[8,512,512]{1,2,0:T(8,128)S(1)}) fusion(f32[8,512]{1,0:T(8,128)S(1)} %get-tuple-element.364, bf16[512,8,64]{0,2,1:T(8,128)(2,1)S(1)} %get-tuple-element.362, bf16[2,512,8,64]{1,3,2,0:T(8,128)(2,1)} %get-tuple-element.363), kind=kOutput, calls=%fused_computation.91 | convolution fusion | flops 274722816 | bytes 9469952 | tf_op jit(solution)/shard_map/while/body/eval_jaxpr/cond/branch_1_fun/qhd,khd->hqk/dot_general | solution.py:69
  205.2 1.8 fusion.110
  207.0 3.9 %conditional.41 = ((f32[512,8,64]{0,2,1:T(8,128)S(1)}, f32[8,512]{1,0:T(8,128)S(1)})) conditional(s32[]{:T(128)} %bitcast.170, (f32[512,8,64]{0,2,1:T(8,128)S(1)}, f32[8,512]{1,0:T(8,128)S(1)}) %get-tuple-element.657, (bf16[2,512,8,64]{1,3,2,0:T(8,128)(2,1)S(1)}, bf16[512,8,64]{0,2,1:T(8,128)(2,1)S(1)}, f32[8,512]{1,0:T(8,128)S(1)}, ...), branch_computations={%region_40.40_spmd, %region_41.42_spmd} | conditional | flops 549715968 | bytes 20545560 | solution.py:103
  207.1 2.0 fusion.119
  209.1 1.8 fusion.128
  213.4 5.5 %constant_dynamic-slice_fusion.10 = (bf16[2,512,512]{1,2,0:T(8,128)(2,1)S(1)}, bf16[2,512,512]{1,2,0:T(8,128)(2,1)}, bf16[2,512,512]{1,2,0:T(8,128)(2,1)}, bf16[...) fusion(bf16[2,5120,512]{1,2,0:T(8,128)(2,1)} %get-tuple-element, ...), kind=kLoop, calls=%fused_computation.120.clone.1 | loop fusion | bytes 14680092 | tf_op jit(solution)/shard_map/while/body/eval_jaxpr/dynamic_slice | solution.py:64
  224.0 2.4 conditional.29
  224.0 2.3 multiply_reduce_fusion.1
  227.0 2.4 conditional.30
  227.0 2.3 multiply_reduce_fusion.2
  229.9 2.4 conditional.31
  229.9 2.3 multiply_reduce_fusion.3
  234.3 3.6 %conditional.35 = (f32[512,8,64]{0,2,1:T(8,128)S(1)}, f32[8,512]{1,0:T(8,128)S(1)}) conditional(s32[]{:T(128)} %bitcast.176, () %tuple.155, (bf16[2,512,8,64]{1,3,2,0:T(8,128)(2,1)S(1)}, bf16[512,8,64]{0,2,1:T(8,128)(2,1)S(1)}, f32[8,512]{1,0:T(8,128)S(1)}) %tuple.229), branch_computations={%region_22.22_spmd, %region_23.24_spmd} | conditional | flops 549449728 | bytes 19447824 | solution.py:103
  234.3 2.0 fusion.14
  237.9 4.8 %conditional.36 = ((f32[512,8,64]{0,2,1:T(8,128)S(1)}, f32[8,512]{1,0:T(8,128)S(1)})) conditional(s32[]{:T(128)} %bitcast.175, (f32[512,8,64]{0,2,1:T(8,128)S(1)}, f32[8,512]{1,0:T(8,128)S(1)}) %conditional.35, (bf16[2,512,8,64]{1,3,2,0:T(8,128)(2,1)}, bf16[512,8,64]{0,2,1:T(8,128)(2,1)S(1)}, f32[8,512]{1,0:T(8,128)S(1)}, ...), branch_computations={%region_25.25_spmd, %region_26.27_spmd} | conditional | flops 549715968 | bytes 24739892 | solution.py:103
  237.9 3.0 %fusion.29 = (f32[8,512]{1,0:T(8,128)S(1)}, f32[8,512,512]{1,2,0:T(8,128)S(1)}) fusion(f32[8,512]{1,0:T(8,128)S(1)} %get-tuple-element.344, bf16[512,8,64]{0,2,1:T(8,128)(2,1)S(1)} %get-tuple-element.342, bf16[2,512,8,64]{1,3,2,0:T(8,128)(2,1)} %get-tuple-element.343), kind=kOutput, calls=%fused_computation.35 | convolution fusion | flops 274722816 | bytes 9469952 | tf_op jit(solution)/shard_map/while/body/eval_jaxpr/cond/branch_1_fun/qhd,khd->hqk/dot_general | solution.py:69
  241.0 1.8 fusion.38
  242.8 3.9 %conditional.37 = ((f32[512,8,64]{0,2,1:T(8,128)S(1)}, f32[8,512]{1,0:T(8,128)S(1)})) conditional(s32[]{:T(128)} %bitcast.174, (f32[512,8,64]{0,2,1:T(8,128)S(1)}, f32[8,512]{1,0:T(8,128)S(1)}) %get-tuple-element.653, (bf16[2,512,8,64]{1,3,2,0:T(8,128)(2,1)S(1)}, bf16[512,8,64]{0,2,1:T(8,128)(2,1)S(1)}, f32[8,512]{1,0:T(8,128)S(1)}, ...), branch_computations={%region_28.28_spmd, %region_29.30_spmd} | conditional | flops 549715968 | bytes 20545560 | solution.py:103
  242.8 2.0 fusion.47
  244.8 1.8 fusion.56
  246.6 4.8 %conditional.38 = ((f32[512,8,64]{0,2,1:T(8,128)S(1)}, f32[8,512]{1,0:T(8,128)S(1)})) conditional(s32[]{:T(128)} %bitcast.173, (f32[512,8,64]{0,2,1:T(8,128)S(1)}, f32[8,512]{1,0:T(8,128)S(1)}) %get-tuple-element.654, (bf16[2,512,8,64]{1,3,2,0:T(8,128)(2,1)}, bf16[512,8,64]{0,2,1:T(8,128)(2,1)S(1)}, f32[8,512]{1,0:T(8,128)S(1)}, ...), branch_computations={%region_31.31_spmd, %region_32.33_spmd} | conditional | flops 549715968 | bytes 24739892 | solution.py:103
  246.7 3.0 %fusion.65 = (f32[8,512]{1,0:T(8,128)S(1)}, f32[8,512,512]{1,2,0:T(8,128)S(1)}) fusion(f32[8,512]{1,0:T(8,128)S(1)} %get-tuple-element.354, bf16[512,8,64]{0,2,1:T(8,128)(2,1)S(1)} %get-tuple-element.352, bf16[2,512,8,64]{1,3,2,0:T(8,128)(2,1)} %get-tuple-element.353), kind=kOutput, calls=%fused_computation.63 | convolution fusion | flops 274722816 | bytes 9469952 | tf_op jit(solution)/shard_map/while/body/eval_jaxpr/cond/branch_1_fun/qhd,khd->hqk/dot_general | solution.py:69
  249.7 1.8 fusion.74
  253.9 17.9 %all_to_all.70 = bf16[4,256,512]{2,1,0:T(8,128)(2,1)S(1)} all-to-all(bf16[4,256,512]{2,1,0:T(8,128)(2,1)} %bitcast.225), channel_id=1, replica_groups=mesh['grp'=2,'ctx'=4,'head'=2,'rep'=2] {'head','rep'}, dimensions={0} | all-to-all | bytes 2097152 | tf_op jit(solution)/shard_map/all_to_all | solution.py:116
  (94 shorter events, 23.5 us)
Async XLA Ops:
  2.3 17.9 %all-to-all-start = ((bf16[256,4,512]{0,2,1:T(8,128)(2,1)}), bf16[256,4,512]{0,2,1:T(8,128)(2,1)S(1)}, u32[]{:S(2)}, u32[]{:S(2)}) async-start(bf16[256,4,512]{0,2,1:T(8,128)(2,1)} %bitcast.46), calls=%async_computation | async-start | bytes 2097152 | tf_op jit(solution)/shard_map/all_to_all | solution.py:21
  5.8 93.9 %copy-start.7 = (s32[8,8]{1,0:T(8,128)S(1)}, s32[8,8]{1,0:T(8,128)}, u32[]{:S(2)}) copy-start(s32[8,8]{1,0:T(8,128)} %param.38) | copy-start | bytes 772
  5.8 93.9 %copy-start.8 = (s32[8]{0:T(128)S(1)}, s32[8]{0:T(128)}, u32[]{:S(2)}) copy-start(s32[8]{0:T(128)} %param.39) | copy-start | bytes 100
  20.2 17.9 %all-to-all-start.1 = ((bf16[256,4,512]{0,2,1:T(8,128)(2,1)}), bf16[256,4,512]{0,2,1:T(8,128)(2,1)S(1)}, u32[]{:S(2)}, u32[]{:S(2)}) async-start(bf16[256,4,512]{0,2,1:T(8,128)(2,1)} %bitcast.49), calls=%async_computation.1 | async-start | bytes 2097152 | tf_op jit(solution)/shard_map/all_to_all | solution.py:22
  38.9 49.1 %collective-permute-start = (bf16[2,1024,512]{2,1,0:T(8,128)(2,1)S(1)}, bf16[2,1024,512]{2,1,0:T(8,128)(2,1)}, u32[]{:S(2)}, u32[]{:S(2)}) collective-permute-start(bf16[2,1024,512]{2,1,0:T(8,128)(2,1)S(1)} %pad_maximum_fusion), channel_id=1, source_target_pairs={{0,4},{4,8},{8,12},{1,5},{5,9},{9,13},{2,6},{6,10},{10,14},{3,7},{... | collective-permute-start | bytes 6291464 | tf_op jit(solution)/shard_map/ppermute | solution.py:15
  42.3 49.1 %collective-permute-start.2 = (bf16[2,1024,512]{2,1,0:T(8,128)(2,1)S(1)}, bf16[2,1024,512]{2,1,0:T(8,128)(2,1)}, u32[]{:S(2)}, u32[]{:S(2)}) collective-permute-start(bf16[2,1024,512]{2,1,0:T(8,128)(2,1)S(1)} %pad_maximum_fusion), channel_id=1, source_target_pairs={{4,0},{8,4},{12,8},{5,1},{9,5},{13,9},{6,2},{10,6},{14,10},{7,3},{... | collective-permute-start | bytes 6291464 | tf_op jit(solution)/shard_map/ppermute | solution.py:15
  87.9 48.4 %collective-permute-start.1 = (bf16[2,1024,512]{2,1,0:T(8,128)(2,1)}, bf16[2,1024,512]{2,1,0:T(8,128)(2,1)}, u32[]{:S(2)}, u32[]{:S(2)}) collective-permute-start(bf16[2,1024,512]{2,1,0:T(8,128)(2,1)} %collective-permute-done), channel_id=1, source_target_pairs={{0,4},{4,8},{8,12},{1,5},{5,9},{9,13},{2,6},{6,10},{10,14},{3,7},{... | collective-permute-start | bytes 6291464 | tf_op jit(solution)/shard_map/ppermute | solution.py:15
  91.4 55.6 %collective-permute-start.3 = (bf16[2,1024,512]{2,1,0:T(8,128)(2,1)}, bf16[2,1024,512]{2,1,0:T(8,128)(2,1)}, u32[]{:S(2)}, u32[]{:S(2)}) collective-permute-start(bf16[2,1024,512]{2,1,0:T(8,128)(2,1)} %collective-permute-done.2), channel_id=1, source_target_pairs={{4,0},{8,4},{12,8},{5,1},{9,5},{13,9},{6,2},{10,6},{14,10},{7,3},{... | collective-permute-start | bytes 6291464 | tf_op jit(solution)/shard_map/ppermute | solution.py:15
  96.1 17.9 %all-to-all-start.2 = ((bf16[256,4,512]{0,2,1:T(8,128)(2,1)}), bf16[256,4,512]{0,2,1:T(8,128)(2,1)S(1)}, u32[]{:S(2)}, u32[]{:S(2)}) async-start(bf16[256,4,512]{0,2,1:T(8,128)(2,1)} %bitcast.222), calls=%async_computation.2 | async-start | bytes 2097152 | tf_op jit(solution)/shard_map/all_to_all | solution.py:20
  170.7 16.3 %copy-start = (bf16[2,512,512]{1,2,0:T(8,128)(2,1)}, bf16[2,512,512]{1,2,0:T(8,128)(2,1)S(1)}, u32[]{:S(2)}) copy-start(bf16[2,512,512]{1,2,0:T(8,128)(2,1)S(1)} %get-tuple-element.528) | copy-start | bytes 3145732 | tf_op jit(solution)/shard_map/while
  188.6 4.9 %copy-start.5 = (bf16[2,512,512]{1,2,0:T(8,128)(2,1)S(1)}, bf16[2,512,512]{1,2,0:T(8,128)(2,1)}, u32[]{:S(2)}) copy-start(bf16[2,512,512]{1,2,0:T(8,128)(2,1)} %get-tuple-element.524) | copy-start | bytes 3145732 | tf_op jit(solution)/shard_map/while
  188.6 3.0 %copy-start.6 = (bf16[2,512,8,64]{1,3,2,0:T(8,128)(2,1)S(1)}, bf16[2,512,8,64]{1,3,2,0:T(8,128)(2,1)}, u32[]{:S(2)}) copy-start(bf16[2,512,8,64]{1,3,2,0:T(8,128)(2,1)} %get-tuple-element.343) | copy-start | bytes 3145732 | tf_op jit(solution)/shard_map/while/body/eval_jaxpr/cond
  193.5 4.9 %copy-start.3 = (bf16[2,512,512]{1,2,0:T(8,128)(2,1)S(1)}, bf16[2,512,512]{1,2,0:T(8,128)(2,1)}, u32[]{:S(2)}) copy-start(bf16[2,512,512]{1,2,0:T(8,128)(2,1)} %get-tuple-element.526) | copy-start | bytes 3145732 | tf_op jit(solution)/shard_map/while
  193.5 3.0 %copy-start.4 = (bf16[2,512,8,64]{1,3,2,0:T(8,128)(2,1)S(1)}, bf16[2,512,8,64]{1,3,2,0:T(8,128)(2,1)}, u32[]{:S(2)}) copy-start(bf16[2,512,8,64]{1,3,2,0:T(8,128)(2,1)} %get-tuple-element.353) | copy-start | bytes 3145732 | tf_op jit(solution)/shard_map/while/body/eval_jaxpr/cond
  202.2 4.9 %copy-start.1 = (bf16[2,512,512]{1,2,0:T(8,128)(2,1)S(1)}, bf16[2,512,512]{1,2,0:T(8,128)(2,1)}, u32[]{:S(2)}) copy-start(bf16[2,512,512]{1,2,0:T(8,128)(2,1)} %copy-done) | copy-start | bytes 3145732 | tf_op jit(solution)/shard_map/while
  202.2 3.0 %copy-start.2 = (bf16[2,512,8,64]{1,3,2,0:T(8,128)(2,1)S(1)}, bf16[2,512,8,64]{1,3,2,0:T(8,128)(2,1)}, u32[]{:S(2)}) copy-start(bf16[2,512,8,64]{1,3,2,0:T(8,128)(2,1)} %get-tuple-element.363) | copy-start | bytes 3145732 | tf_op jit(solution)/shard_map/while/body/eval_jaxpr/cond
  219.0 15.3 %copy-start = (bf16[2,512,512]{1,2,0:T(8,128)(2,1)}, bf16[2,512,512]{1,2,0:T(8,128)(2,1)S(1)}, u32[]{:S(2)}) copy-start(bf16[2,512,512]{1,2,0:T(8,128)(2,1)S(1)} %get-tuple-element.528) | copy-start | bytes 3145732 | tf_op jit(solution)/shard_map/while
  237.9 4.9 %copy-start.5 = (bf16[2,512,512]{1,2,0:T(8,128)(2,1)S(1)}, bf16[2,512,512]{1,2,0:T(8,128)(2,1)}, u32[]{:S(2)}) copy-start(bf16[2,512,512]{1,2,0:T(8,128)(2,1)} %get-tuple-element.524) | copy-start | bytes 3145732 | tf_op jit(solution)/shard_map/while
  237.9 3.0 %copy-start.6 = (bf16[2,512,8,64]{1,3,2,0:T(8,128)(2,1)S(1)}, bf16[2,512,8,64]{1,3,2,0:T(8,128)(2,1)}, u32[]{:S(2)}) copy-start(bf16[2,512,8,64]{1,3,2,0:T(8,128)(2,1)} %get-tuple-element.343) | copy-start | bytes 3145732 | tf_op jit(solution)/shard_map/while/body/eval_jaxpr/cond
  246.6 4.9 %copy-start.3 = (bf16[2,512,512]{1,2,0:T(8,128)(2,1)S(1)}, bf16[2,512,512]{1,2,0:T(8,128)(2,1)}, u32[]{:S(2)}) copy-start(bf16[2,512,512]{1,2,0:T(8,128)(2,1)} %get-tuple-element.526) | copy-start | bytes 3145732 | tf_op jit(solution)/shard_map/while
  246.7 3.0 %copy-start.4 = (bf16[2,512,8,64]{1,3,2,0:T(8,128)(2,1)S(1)}, bf16[2,512,8,64]{1,3,2,0:T(8,128)(2,1)}, u32[]{:S(2)}) copy-start(bf16[2,512,8,64]{1,3,2,0:T(8,128)(2,1)} %get-tuple-element.353) | copy-start | bytes 3145732 | tf_op jit(solution)/shard_map/while/body/eval_jaxpr/cond
  251.5 1.2 copy-start.1
where the time goes:
time: 275 us; the launch traced here: 274 us
  waiting for transfers between devices  104 us (38%)
  matrix products  58.5 us (21%)
  local copies, waits for them, and re-layouts  57.8 us (21%)
  starting transfers between devices  22.2 us (8%)
  blocking collectives  17.9 us (7%)
  loops' own time  11.2 us (4%)
    ppermute x4, waiting for transfers between devices, from_behind(): return lax.ppermute(x, axis, pairs)  64.2 us
    dot_general x18, matrix products, block_scores(): jnp.einsum('qhd,khd->hqk', query_tile, kv_block[0], preferred_element_typ...  42.2 us
    all_to_all x1, blocking collectives, shards(): lax.all_to_all(attended, ('head', 'rep'), split_axis=0, concat_axis=1, ti...  17.9 us
    unnamed x10, local copies, waits for them, and re-layouts  16 us
    dot_general x9, matrix products, add_weights(): jnp.einsum('hqk,khd->qhd', rounded, value_block, preferred_element_type=j...  15.7 us
    all_to_all x1, waiting for transfers between devices, shards(): lax.all_to_all(values, ('head', 'rep'), split_axis=1, concat_axis=0, tile...  13.8 us
    all_to_all x1, waiting for transfers between devices, shards(): lax.all_to_all(queries, ('head', 'rep'), split_axis=1, concat_axis=0, til...  13.8 us
    while x1, local copies, waits for them, and re-layouts, shards(): tiles_out = lax.map(attend_tile, jnp.arange(tile_count, dtype=jnp.int32))  13.8 us
  transfers between devices with their start and end apart: 7, of which 5 were waited for; matrix products, arithmetic and copies ran while one was open for 6% of the time, Pallas kernels for 0%

commit v1 on v0

--- a/solution.py
+++ b/solution.py
@@ -16,10 +16,28 @@
 
 
 def shards(queries, keys, values, reads, owner):
+
+    def draft_the_sides(base_x):
+        left_arr, now = (jax.lax.axis_size(("head", "rep")), jax.lax.axis_index(("head", "rep")))
+        taken_in = base_x.shape[1] // left_arr
+        piece_now = jnp.roll(base_x, -now * taken_in, 1)
+        so_far_all = [lax.slice_in_dim(piece_now, 0, taken_in, axis=1)]
+        for dev in range(1, left_arr):
+            local_out = lax.slice_in_dim(piece_now, dev * taken_in, (dev + 1) * taken_in, axis=1)
+            so_far_all.append(
+                jax.lax.ppermute(
+                    local_out,
+                    axis_name=("head", "rep"),
+                    perm=[(ii, (ii + dev) % left_arr) for ii in range(left_arr)],
+                )
+            )
+        arr_now = jnp.concatenate(so_far_all[::-1], 0)
+        return jnp.roll(arr_now, (now + 1) * so_far_all[0].shape[0], axis=0)
+
     query_heads, key_heads, value_heads = (
         lax.all_to_all(queries, ("head", "rep"), split_axis=1, concat_axis=0, tiled=True),
         lax.all_to_all(keys, ("head", "rep"), split_axis=1, concat_axis=0, tiled=True),
-        lax.all_to_all(values, ("head", "rep"), split_axis=1, concat_axis=0, tiled=True),
+        draft_the_sides(values),
     )
     row_count, feat_width = query_heads.shape
     heads_dev = feat_width // HEAD_DIM

time: 275 us -> 267 us (0.971)
  waiting for transfers between devices: 104 us -> 96.7 us
    all_to_all x1 -> x0, waiting for transfers between devices: 13.8 us -> none  [shards(): lax.all_to_all(values, ('head', 'rep'), split_axis=1, concat_axis=0, tile...]
    ppermute x0 -> x3, waiting for transfers between devices: none -> 6.91 us  [draft_the_sides(): jax.lax.ppermute(local_out, axis_name=('head', 'rep'), perm=[(ii, (ii + d...]
    all_to_all x1 -> x0, starting transfers between devices: 3.52 us -> none  [shards(): lax.all_to_all(values, ('head', 'rep'), split_axis=1, concat_axis=0, tile...]
    unnamed x10 -> x16, local copies, waits for them, and re-layouts: 16 us -> 13.9 us
  transfers between devices with their start and end apart: 7 -> 9, of which waited for: 5 -> 6; matrix products, arithmetic and copies ran while one was open for 6% -> 7% of each run, Pallas kernels for 0% -> 0%
where the time goes in v1:
time: 267 us; the launch traced here: 265 us
  waiting for transfers between devices  96.7 us (36%)
  matrix products  58.5 us (22%)
  local copies, waits for them, and re-layouts  56.3 us (21%)
  starting transfers between devices  20.4 us (8%)
  blocking collectives  17.9 us (7%)
  loops' own time  11.3 us (4%)
  other arithmetic  3.69 us (1%)
    ppermute x4, waiting for transfers between devices, from_behind(): return lax.ppermute(x, axis, pairs)  65.1 us
    dot_general x18, matrix products, block_scores(): jnp.einsum('qhd,khd->hqk', query_tile, kv_block[0], preferred_element_typ...  42.2 us
    all_to_all x1, blocking collectives, shards(): lax.all_to_all(attended, ('head', 'rep'), split_axis=0, concat_axis=1, ti...  17.9 us
    dot_general x9, matrix products, add_weights(): jnp.einsum('hqk,khd->qhd', rounded, value_block, preferred_element_type=j...  15.7 us
    unnamed x16, local copies, waits for them, and re-layouts  13.9 us
    while x1, local copies, waits for them, and re-layouts, shards(): tiles_out = lax.map(attend_tile, jnp.arange(tile_count, dtype=jnp.int32))  13.9 us
    all_to_all x1, waiting for transfers between devices, shards(): lax.all_to_all(queries, ('head', 'rep'), split_axis=1, concat_axis=0, til...  13.8 us
    ppermute x4, starting transfers between devices, from_behind(): return lax.ppermute(x, axis, pairs)  11.7 us
  transfers between devices with their start and end apart: 9, of which 6 were waited for; matrix products, arithmetic and copies ran while one was open for 7% of the time, Pallas kernels for 0%

profile of v1, /device:TPU:20, one launch (start us, length us, event | category | flops | bytes accessed | tf_op | source)
XLA Modules:
  0.0 264.9 jit_solution(12173346184395723188)
XLA Ops:
  0.0 1.6 fusion.137
  4.1 2.3 copy.60
  6.3 3.5 %all-to-all-start = ((bf16[256,4,512]{0,2,1:T(8,128)(2,1)}), bf16[256,4,512]{0,2,1:T(8,128)(2,1)S(1)}, u32[]{:S(2)}, u32[]{:S(2)}) async-start(bf16[256,4,512]{0,2,1:T(8,128)(2,1)} %bitcast.46), calls=%async_computation | async-start | bytes 2097152 | tf_op jit(solution)/shard_map/all_to_all | solution.py:39
  10.3 6.5 %collective-permute-done.1 = bf16[256,512]{1,0:T(8,128)(2,1)S(1)} collective-permute-done((bf16[256,512]{1,0:T(8,128)(2,1)S(1)}, bf16[256,512]{1,0:T(8,128)(2,1)S(1)}, u32[]{:S(2)}, u32[]{:S(2)}) %collective-permute-start.1) | collective-permute-done | bytes 262176 | tf_op jit(solution)/shard_map/ppermute | solution.py:28
  17.1 10.8 %all-to-all-done = bf16[256,4,512]{0,2,1:T(8,128)(2,1)S(1)} async-done(((bf16[256,4,512]{0,2,1:T(8,128)(2,1)}), bf16[256,4,512]{0,2,1:T(8,128)(2,1)S(1)}, u32[]{:S(2)}, u32[]{:S(2)}) %all-to-all-start) | async-done | bytes 1048608 | tf_op jit(solution)/shard_map/all_to_all | solution.py:39
  28.7 3.5 %collective-permute-start.3 = (bf16[2,1024,512]{2,1,0:T(8,128)(2,1)S(1)}, bf16[2,1024,512]{2,1,0:T(8,128)(2,1)}, u32[]{:S(2)}, u32[]{:S(2)}) collective-permute-start(bf16[2,1024,512]{2,1,0:T(8,128)(2,1)S(1)} %pad_maximum_fusion), channel_id=1, source_target_pairs={{0,4},{4,8},{8,12},{1,5},{5,9},{9,13},{2,6},{6,10},{10,14},{3,7},{... | collective-permute-start | bytes 6291464 | tf_op jit(solution)/shard_map/ppermute | solution.py:15
  32.2 2.4 collective-permute-start.5
  34.6 43.7 %collective-permute-done.3 = bf16[2,1024,512]{2,1,0:T(8,128)(2,1)} collective-permute-done((bf16[2,1024,512]{2,1,0:T(8,128)(2,1)S(1)}, bf16[2,1024,512]{2,1,0:T(8,128)(2,1)}, u32[]{:S(2)}, u32[]{:S(2)}) %collective-permute-start.3) | collective-permute-done | bytes 2097184 | tf_op jit(solution)/shard_map/ppermute | solution.py:15
  78.2 3.5 %collective-permute-start.4 = (bf16[2,1024,512]{2,1,0:T(8,128)(2,1)}, bf16[2,1024,512]{2,1,0:T(8,128)(2,1)}, u32[]{:S(2)}, u32[]{:S(2)}) collective-permute-start(bf16[2,1024,512]{2,1,0:T(8,128)(2,1)} %collective-permute-done.3), channel_id=1, source_target_pairs={{0,4},{4,8},{8,12},{1,5},{5,9},{9,13},{2,6},{6,10},{10,14},{3,7},{... | collective-permute-start | bytes 6291464 | tf_op jit(solution)/shard_map/ppermute | solution.py:15
  81.7 2.4 collective-permute-start.6
  84.1 2.3 copy.62
  86.4 3.5 %all-to-all-start.1 = ((bf16[256,4,512]{0,2,1:T(8,128)(2,1)}), bf16[256,4,512]{0,2,1:T(8,128)(2,1)S(1)}, u32[]{:S(2)}, u32[]{:S(2)}) async-start(bf16[256,4,512]{0,2,1:T(8,128)(2,1)} %bitcast.218), calls=%async_computation.1 | async-start | bytes 2097152 | tf_op jit(solution)/shard_map/all_to_all | solution.py:38
  90.5 13.8 %all-to-all-done.1 = bf16[256,4,512]{0,2,1:T(8,128)(2,1)S(1)} async-done(((bf16[256,4,512]{0,2,1:T(8,128)(2,1)}), bf16[256,4,512]{0,2,1:T(8,128)(2,1)S(1)}, u32[]{:S(2)}, u32[]{:S(2)}) %all-to-all-start.1) | async-done | bytes 1048608 | tf_op jit(solution)/shard_map/all_to_all | solution.py:38
  105.7 21.5 %collective-permute-done.4 = bf16[2,1024,512]{2,1,0:T(8,128)(2,1)} collective-permute-done((bf16[2,1024,512]{2,1,0:T(8,128)(2,1)}, bf16[2,1024,512]{2,1,0:T(8,128)(2,1)}, u32[]{:S(2)}, u32[]{:S(2)}) %collective-permute-start.4) | collective-permute-done | bytes 2097184 | tf_op jit(solution)/shard_map/ppermute | solution.py:15
  127.1 3.1 %constant_dynamic-update-slice_fusion.11 = bf16[2,5120,512]{2,1,0:T(8,128)(2,1)} fusion(bf16[2,1024,512]{2,1,0:T(8,128)(2,1)} %collective-permute-done.4), kind=kLoop, calls=%fused_computation.145 | loop fusion | bytes 4194304
  130.2 3.1 %constant_dynamic-update-slice_fusion.10 = bf16[2,5120,512]{2,1,0:T(8,128)(2,1)} fusion(bf16[2,5120,512]{2,1,0:T(8,128)(2,1)} %constant_dynamic-update-slice_fusion.11, bf16[2,1024,512]{2,1,0:T(8,128)(2,1)} %collective-permute-done.3), kind=kLoop, calls=%fused_computation.144 | loop fusion | bytes 4194304
  134.8 3.0 %constant_dynamic-update-slice_fusion.8 = bf16[2,5120,512]{2,1,0:T(8,128)(2,1)} fusion(bf16[2,5120,512]{2,1,0:T(8,128)(2,1)} %constant_dynamic-update-slice_fusion.9, bf16[2,1024,512]{2,1,0:T(8,128)(2,1)} %collective-permute-done.5), kind=kLoop, calls=%fused_computation.142 | loop fusion | bytes 4194304
  137.8 3.1 %constant_dynamic-update-slice_fusion.7 = bf16[2,5120,512]{2,1,0:T(8,128)(2,1)} fusion(bf16[2,5120,512]{2,1,0:T(8,128)(2,1)} %constant_dynamic-update-slice_fusion.8, bf16[2,1024,512]{2,1,0:T(8,128)(2,1)} %collective-permute-done.6), kind=kLoop, calls=%fused_computation.141 | loop fusion | bytes 4194304 | tf_op jit(solution)/shard_map/concatenate | solution.py:58
  140.9 13.9 %copy.64 = bf16[2,5120,512]{1,2,0:T(8,128)(2,1)} copy(bf16[2,5120,512]{2,1,0:T(8,128)(2,1)} %constant_dynamic-update-slice_fusion.7) | data formatting | bytes 20971520 | tf_op jit(solution)/shard_map/while | solution.py:132
  154.8 90.3 %while.13 = (s32[]{:T(128)}, bf16[2,512,512]{2,1,0:T(8,128)(2,1)}, s32[2]{0:T(128)S(1)}, s32[]{:T(128)}, f32[14,8]{0,1:T(8,128)S(1)}, /*index=5*/bf16[2,5120,512...) while((s32[]{:T(128)}, bf16[2,512,512]{2,1,0:T(8,128)(2,1)}, ...), condition=%wide.region_43.44_spmd, body=%wide.region_0.43_spmd.sunk | while | flops 5756674048 | bytes 200296880 | solution.py:132
  156.2 5.6 %constant_dynamic-slice_fusion.10 = (bf16[2,512,512]{1,2,0:T(8,128)(2,1)S(1)}, bf16[2,512,512]{1,2,0:T(8,128)(2,1)}, bf16[2,512,512]{1,2,0:T(8,128)(2,1)}, bf16[...) fusion(bf16[2,5120,512]{1,2,0:T(8,128)(2,1)} %get-tuple-element, ...), kind=kLoop, calls=%fused_computation.120.clone.1 | loop fusion | bytes 14680092 | tf_op jit(solution)/shard_map/while/body/eval_jaxpr/dynamic_slice | solution.py:82
  165.4 2.4 conditional.29
  165.5 2.3 multiply_reduce_fusion.1
  169.2 2.4 conditional.31
  169.2 2.3 multiply_reduce_fusion.3
  172.1 2.4 conditional.32
  172.1 2.3 multiply_reduce_fusion.4
  175.0 2.4 conditional.33
  175.0 2.3 multiply_reduce_fusion.5
  179.6 4.8 %conditional.36 = ((f32[512,8,64]{0,2,1:T(8,128)S(1)}, f32[8,512]{1,0:T(8,128)S(1)})) conditional(s32[]{:T(128)} %bitcast.173, (f32[512,8,64]{0,2,1:T(8,128)S(1)}, f32[8,512]{1,0:T(8,128)S(1)}) %conditional.35, (bf16[2,512,8,64]{1,3,2,0:T(8,128)(2,1)}, bf16[512,8,64]{0,2,1:T(8,128)(2,1)S(1)}, f32[8,512]{1,0:T(8,128)S(1)}, ...), branch_computations={%region_25.25_spmd, %region_26.27_spmd} | conditional | flops 549715968 | bytes 24739892 | solution.py:121
  179.6 3.0 %fusion.29 = (f32[8,512]{1,0:T(8,128)S(1)}, f32[8,512,512]{1,2,0:T(8,128)S(1)}) fusion(f32[8,512]{1,0:T(8,128)S(1)} %get-tuple-element.344, bf16[512,8,64]{0,2,1:T(8,128)(2,1)S(1)} %get-tuple-element.342, bf16[2,512,8,64]{1,3,2,0:T(8,128)(2,1)} %get-tuple-element.343), kind=kOutput, calls=%fused_computation.35 | convolution fusion | flops 274722816 | bytes 9469952 | tf_op jit(solution)/shard_map/while/body/eval_jaxpr/cond/branch_1_fun/qhd,khd->hqk/dot_general | solution.py:87
  182.6 1.8 fusion.38
  184.5 4.8 %conditional.38 = ((f32[512,8,64]{0,2,1:T(8,128)S(1)}, f32[8,512]{1,0:T(8,128)S(1)})) conditional(s32[]{:T(128)} %bitcast.171, (f32[512,8,64]{0,2,1:T(8,128)S(1)}, f32[8,512]{1,0:T(8,128)S(1)}) %get-tuple-element.657, (bf16[2,512,8,64]{1,3,2,0:T(8,128)(2,1)}, bf16[512,8,64]{0,2,1:T(8,128)(2,1)S(1)}, f32[8,512]{1,0:T(8,128)S(1)}, ...), branch_computations={%region_31.31_spmd, %region_32.33_spmd} | conditional | flops 549715968 | bytes 24739892 | solution.py:121
  184.5 3.0 %fusion.65 = (f32[8,512]{1,0:T(8,128)S(1)}, f32[8,512,512]{1,2,0:T(8,128)S(1)}) fusion(f32[8,512]{1,0:T(8,128)S(1)} %get-tuple-element.354, bf16[512,8,64]{0,2,1:T(8,128)(2,1)S(1)} %get-tuple-element.352, bf16[2,512,8,64]{1,3,2,0:T(8,128)(2,1)} %get-tuple-element.353), kind=kOutput, calls=%fused_computation.63 | convolution fusion | flops 274722816 | bytes 9469952 | tf_op jit(solution)/shard_map/while/body/eval_jaxpr/cond/branch_1_fun/qhd,khd->hqk/dot_general | solution.py:87
  187.5 1.8 fusion.74
  189.3 3.9 %conditional.39 = ((f32[512,8,64]{0,2,1:T(8,128)S(1)}, f32[8,512]{1,0:T(8,128)S(1)})) conditional(s32[]{:T(128)} %bitcast.170, (f32[512,8,64]{0,2,1:T(8,128)S(1)}, f32[8,512]{1,0:T(8,128)S(1)}) %get-tuple-element.658, (bf16[2,512,8,64]{1,3,2,0:T(8,128)(2,1)S(1)}, bf16[512,8,64]{0,2,1:T(8,128)(2,1)S(1)}, f32[8,512]{1,0:T(8,128)S(1)}, ...), branch_computations={%region_34.34_spmd, %region_35.36_spmd} | conditional | flops 549715968 | bytes 20545560 | solution.py:121
  189.3 2.0 fusion.83
  191.4 1.8 fusion.92
  193.2 4.8 %conditional.40 = ((f32[512,8,64]{0,2,1:T(8,128)S(1)}, f32[8,512]{1,0:T(8,128)S(1)})) conditional(s32[]{:T(128)} %bitcast.169, (f32[512,8,64]{0,2,1:T(8,128)S(1)}, f32[8,512]{1,0:T(8,128)S(1)}) %get-tuple-element.659, (bf16[2,512,8,64]{1,3,2,0:T(8,128)(2,1)}, bf16[512,8,64]{0,2,1:T(8,128)(2,1)S(1)}, f32[8,512]{1,0:T(8,128)S(1)}, ...), branch_computations={%region_37.37_spmd, %region_38.39_spmd} | conditional | flops 549715968 | bytes 24739892 | solution.py:121
  193.2 3.0 %fusion.101 = (f32[8,512]{1,0:T(8,128)S(1)}, f32[8,512,512]{1,2,0:T(8,128)S(1)}) fusion(f32[8,512]{1,0:T(8,128)S(1)} %get-tuple-element.364, bf16[512,8,64]{0,2,1:T(8,128)(2,1)S(1)} %get-tuple-element.362, bf16[2,512,8,64]{1,3,2,0:T(8,128)(2,1)} %get-tuple-element.363), kind=kOutput, calls=%fused_computation.91 | convolution fusion | flops 274722816 | bytes 9469952 | tf_op jit(solution)/shard_map/while/body/eval_jaxpr/cond/branch_1_fun/qhd,khd->hqk/dot_general | solution.py:87
  196.2 1.8 fusion.110
  198.0 3.9 %conditional.41 = ((f32[512,8,64]{0,2,1:T(8,128)S(1)}, f32[8,512]{1,0:T(8,128)S(1)})) conditional(s32[]{:T(128)} %bitcast.168, (f32[512,8,64]{0,2,1:T(8,128)S(1)}, f32[8,512]{1,0:T(8,128)S(1)}) %get-tuple-element.660, (bf16[2,512,8,64]{1,3,2,0:T(8,128)(2,1)S(1)}, bf16[512,8,64]{0,2,1:T(8,128)(2,1)S(1)}, f32[8,512]{1,0:T(8,128)S(1)}, ...), branch_computations={%region_40.40_spmd, %region_41.42_spmd} | conditional | flops 549715968 | bytes 20545560 | solution.py:121
  198.1 2.0 fusion.119
  200.1 1.8 fusion.128
  204.5 5.6 %constant_dynamic-slice_fusion.10 = (bf16[2,512,512]{1,2,0:T(8,128)(2,1)S(1)}, bf16[2,512,512]{1,2,0:T(8,128)(2,1)}, bf16[2,512,512]{1,2,0:T(8,128)(2,1)}, bf16[...) fusion(bf16[2,5120,512]{1,2,0:T(8,128)(2,1)} %get-tuple-element, ...), kind=kLoop, calls=%fused_computation.120.clone.1 | loop fusion | bytes 14680092 | tf_op jit(solution)/shard_map/while/body/eval_jaxpr/dynamic_slice | solution.py:82
  215.1 2.4 conditional.29
  215.1 2.3 multiply_reduce_fusion.1
  218.1 2.4 conditional.30
  218.1 2.3 multiply_reduce_fusion.2
  221.2 2.4 conditional.31
  221.2 2.3 multiply_reduce_fusion.3
  225.4 3.6 %conditional.35 = (f32[512,8,64]{0,2,1:T(8,128)S(1)}, f32[8,512]{1,0:T(8,128)S(1)}) conditional(s32[]{:T(128)} %bitcast.174, () %tuple.157, (bf16[2,512,8,64]{1,3,2,0:T(8,128)(2,1)S(1)}, bf16[512,8,64]{0,2,1:T(8,128)(2,1)S(1)}, f32[8,512]{1,0:T(8,128)S(1)}) %tuple.231), branch_computations={%region_22.22_spmd, %region_23.24_spmd} | conditional | flops 549449728 | bytes 19447824 | solution.py:121
  225.4 2.0 fusion.14
  227.5 1.6 fusion.20
  229.0 4.8 %conditional.36 = ((f32[512,8,64]{0,2,1:T(8,128)S(1)}, f32[8,512]{1,0:T(8,128)S(1)})) conditional(s32[]{:T(128)} %bitcast.173, (f32[512,8,64]{0,2,1:T(8,128)S(1)}, f32[8,512]{1,0:T(8,128)S(1)}) %conditional.35, (bf16[2,512,8,64]{1,3,2,0:T(8,128)(2,1)}, bf16[512,8,64]{0,2,1:T(8,128)(2,1)S(1)}, f32[8,512]{1,0:T(8,128)S(1)}, ...), branch_computations={%region_25.25_spmd, %region_26.27_spmd} | conditional | flops 549715968 | bytes 24739892 | solution.py:121
  229.1 3.0 %fusion.29 = (f32[8,512]{1,0:T(8,128)S(1)}, f32[8,512,512]{1,2,0:T(8,128)S(1)}) fusion(f32[8,512]{1,0:T(8,128)S(1)} %get-tuple-element.344, bf16[512,8,64]{0,2,1:T(8,128)(2,1)S(1)} %get-tuple-element.342, bf16[2,512,8,64]{1,3,2,0:T(8,128)(2,1)} %get-tuple-element.343), kind=kOutput, calls=%fused_computation.35 | convolution fusion | flops 274722816 | bytes 9469952 | tf_op jit(solution)/shard_map/while/body/eval_jaxpr/cond/branch_1_fun/qhd,khd->hqk/dot_general | solution.py:87
  232.1 1.8 fusion.38
  233.9 3.9 %conditional.37 = ((f32[512,8,64]{0,2,1:T(8,128)S(1)}, f32[8,512]{1,0:T(8,128)S(1)})) conditional(s32[]{:T(128)} %bitcast.172, (f32[512,8,64]{0,2,1:T(8,128)S(1)}, f32[8,512]{1,0:T(8,128)S(1)}) %get-tuple-element.656, (bf16[2,512,8,64]{1,3,2,0:T(8,128)(2,1)S(1)}, bf16[512,8,64]{0,2,1:T(8,128)(2,1)S(1)}, f32[8,512]{1,0:T(8,128)S(1)}, ...), branch_computations={%region_28.28_spmd, %region_29.30_spmd} | conditional | flops 549715968 | bytes 20545560 | solution.py:121
  233.9 2.0 fusion.47
  236.0 1.8 fusion.56
  237.8 4.8 %conditional.38 = ((f32[512,8,64]{0,2,1:T(8,128)S(1)}, f32[8,512]{1,0:T(8,128)S(1)})) conditional(s32[]{:T(128)} %bitcast.171, (f32[512,8,64]{0,2,1:T(8,128)S(1)}, f32[8,512]{1,0:T(8,128)S(1)}) %get-tuple-element.657, (bf16[2,512,8,64]{1,3,2,0:T(8,128)(2,1)}, bf16[512,8,64]{0,2,1:T(8,128)(2,1)S(1)}, f32[8,512]{1,0:T(8,128)S(1)}, ...), branch_computations={%region_31.31_spmd, %region_32.33_spmd} | conditional | flops 549715968 | bytes 24739892 | solution.py:121
  237.8 3.0 %fusion.65 = (f32[8,512]{1,0:T(8,128)S(1)}, f32[8,512,512]{1,2,0:T(8,128)S(1)}) fusion(f32[8,512]{1,0:T(8,128)S(1)} %get-tuple-element.354, bf16[512,8,64]{0,2,1:T(8,128)(2,1)S(1)} %get-tuple-element.352, bf16[2,512,8,64]{1,3,2,0:T(8,128)(2,1)} %get-tuple-element.353), kind=kOutput, calls=%fused_computation.63 | convolution fusion | flops 274722816 | bytes 9469952 | tf_op jit(solution)/shard_map/while/body/eval_jaxpr/cond/branch_1_fun/qhd,khd->hqk/dot_general | solution.py:87
  240.8 1.8 fusion.74
  245.0 17.9 %all_to_all.54 = bf16[4,256,512]{2,1,0:T(8,128)(2,1)S(1)} all-to-all(bf16[4,256,512]{2,1,0:T(8,128)(2,1)} %bitcast.221), channel_id=1, replica_groups=mesh['grp'=2,'ctx'=4,'head'=2,'rep'=2] {'head','rep'}, dimensions={0} | all-to-all | bytes 2097152 | tf_op jit(solution)/shard_map/all_to_all | solution.py:134
  (107 shorter events, 24.6 us)
Async XLA Ops:
  2.4 7.9 %collective-permute-start = (bf16[256,512]{1,0:T(8,128)(2,1)}, bf16[256,512]{1,0:T(8,128)(2,1)S(1)}, u32[]{:S(2)}, u32[]{:S(2)}) collective-permute-start(bf16[256,512]{1,0:T(8,128)(2,1)} %get-tuple-element.446), channel_id=1, source_target_pairs={{0,3},{1,0},{2,1},{3,2},{4,7},{5,4},{6,5},{7,6},{8,11},{9,8},{10,9... | collective-permute-start | bytes 786440 | tf_op jit(solution)/shard_map/ppermute | solution.py:28
  3.3 13.5 %collective-permute-start.1 = (bf16[256,512]{1,0:T(8,128)(2,1)S(1)}, bf16[256,512]{1,0:T(8,128)(2,1)S(1)}, u32[]{:S(2)}, u32[]{:S(2)}) collective-permute-start(bf16[256,512]{1,0:T(8,128)(2,1)S(1)} %get-tuple-element.445), channel_id=1, source_target_pairs={{0,2},{1,3},{2,0},{3,1},{4,6},{5,7},{6,4},{7,5},{8,10},{9,11},{10,... | collective-permute-start | bytes 786440 | tf_op jit(solution)/shard_map/ppermute | solution.py:28
  3.9 13.0 %collective-permute-start.2 = (bf16[256,512]{1,0:T(8,128)(2,1)S(1)}, bf16[256,512]{1,0:T(8,128)(2,1)S(1)}, u32[]{:S(2)}, u32[]{:S(2)}) collective-permute-start(bf16[256,512]{1,0:T(8,128)(2,1)S(1)} %get-tuple-element.444), channel_id=1, source_target_pairs={{0,1},{1,2},{2,3},{3,0},{4,5},{5,6},{6,7},{7,4},{8,9},{9,10},{10,1... | collective-permute-start | bytes 786440 | tf_op jit(solution)/shard_map/ppermute | solution.py:28
  6.3 21.6 %all-to-all-start = ((bf16[256,4,512]{0,2,1:T(8,128)(2,1)}), bf16[256,4,512]{0,2,1:T(8,128)(2,1)S(1)}, u32[]{:S(2)}, u32[]{:S(2)}) async-start(bf16[256,4,512]{0,2,1:T(8,128)(2,1)} %bitcast.46), calls=%async_computation | async-start | bytes 2097152 | tf_op jit(solution)/shard_map/all_to_all | solution.py:39
  9.9 80.1 %copy-start.7 = (s32[8,8]{1,0:T(8,128)S(1)}, s32[8,8]{1,0:T(8,128)}, u32[]{:S(2)}) copy-start(s32[8,8]{1,0:T(8,128)} %param.38) | copy-start | bytes 772
  9.9 80.1 %copy-start.8 = (s32[8]{0:T(128)S(1)}, s32[8]{0:T(128)}, u32[]{:S(2)}) copy-start(s32[8]{0:T(128)} %param.39) | copy-start | bytes 100
  28.7 49.5 %collective-permute-start.3 = (bf16[2,1024,512]{2,1,0:T(8,128)(2,1)S(1)}, bf16[2,1024,512]{2,1,0:T(8,128)(2,1)}, u32[]{:S(2)}, u32[]{:S(2)}) collective-permute-start(bf16[2,1024,512]{2,1,0:T(8,128)(2,1)S(1)} %pad_maximum_fusion), channel_id=1, source_target_pairs={{0,4},{4,8},{8,12},{1,5},{5,9},{9,13},{2,6},{6,10},{10,14},{3,7},{... | collective-permute-start | bytes 6291464 | tf_op jit(solution)/shard_map/ppermute | solution.py:15
  32.2 49.5 %collective-permute-start.5 = (bf16[2,1024,512]{2,1,0:T(8,128)(2,1)S(1)}, bf16[2,1024,512]{2,1,0:T(8,128)(2,1)}, u32[]{:S(2)}, u32[]{:S(2)}) collective-permute-start(bf16[2,1024,512]{2,1,0:T(8,128)(2,1)S(1)} %pad_maximum_fusion), channel_id=1, source_target_pairs={{4,0},{8,4},{12,8},{5,1},{9,5},{13,9},{6,2},{10,6},{14,10},{7,3},{... | collective-permute-start | bytes 6291464 | tf_op jit(solution)/shard_map/ppermute | solution.py:15
  78.2 48.9 %collective-permute-start.4 = (bf16[2,1024,512]{2,1,0:T(8,128)(2,1)}, bf16[2,1024,512]{2,1,0:T(8,128)(2,1)}, u32[]{:S(2)}, u32[]{:S(2)}) collective-permute-start(bf16[2,1024,512]{2,1,0:T(8,128)(2,1)} %collective-permute-done.3), channel_id=1, source_target_pairs={{0,4},{4,8},{8,12},{1,5},{5,9},{9,13},{2,6},{6,10},{10,14},{3,7},{... | collective-permute-start | bytes 6291464 | tf_op jit(solution)/shard_map/ppermute | solution.py:15
  81.7 56.1 %collective-permute-start.6 = (bf16[2,1024,512]{2,1,0:T(8,128)(2,1)}, bf16[2,1024,512]{2,1,0:T(8,128)(2,1)}, u32[]{:S(2)}, u32[]{:S(2)}) collective-permute-start(bf16[2,1024,512]{2,1,0:T(8,128)(2,1)} %collective-permute-done.5), channel_id=1, source_target_pairs={{4,0},{8,4},{12,8},{5,1},{9,5},{13,9},{6,2},{10,6},{14,10},{7,3},{... | collective-permute-start | bytes 6291464 | tf_op jit(solution)/shard_map/ppermute | solution.py:15
  86.4 17.9 %all-to-all-start.1 = ((bf16[256,4,512]{0,2,1:T(8,128)(2,1)}), bf16[256,4,512]{0,2,1:T(8,128)(2,1)S(1)}, u32[]{:S(2)}, u32[]{:S(2)}) async-start(bf16[256,4,512]{0,2,1:T(8,128)(2,1)} %bitcast.218), calls=%async_computation.1 | async-start | bytes 2097152 | tf_op jit(solution)/shard_map/all_to_all | solution.py:38
  161.7 16.3 %copy-start = (bf16[2,512,512]{1,2,0:T(8,128)(2,1)}, bf16[2,512,512]{1,2,0:T(8,128)(2,1)S(1)}, u32[]{:S(2)}) copy-start(bf16[2,512,512]{1,2,0:T(8,128)(2,1)S(1)} %get-tuple-element.531) | copy-start | bytes 3145732 | tf_op jit(solution)/shard_map/while
  179.6 4.9 %copy-start.5 = (bf16[2,512,512]{1,2,0:T(8,128)(2,1)S(1)}, bf16[2,512,512]{1,2,0:T(8,128)(2,1)}, u32[]{:S(2)}) copy-start(bf16[2,512,512]{1,2,0:T(8,128)(2,1)} %get-tuple-element.527) | copy-start | bytes 3145732 | tf_op jit(solution)/shard_map/while
  179.6 3.0 %copy-start.6 = (bf16[2,512,8,64]{1,3,2,0:T(8,128)(2,1)S(1)}, bf16[2,512,8,64]{1,3,2,0:T(8,128)(2,1)}, u32[]{:S(2)}) copy-start(bf16[2,512,8,64]{1,3,2,0:T(8,128)(2,1)} %get-tuple-element.343) | copy-start | bytes 3145732 | tf_op jit(solution)/shard_map/while/body/eval_jaxpr/cond
  184.5 4.9 %copy-start.3 = (bf16[2,512,512]{1,2,0:T(8,128)(2,1)S(1)}, bf16[2,512,512]{1,2,0:T(8,128)(2,1)}, u32[]{:S(2)}) copy-start(bf16[2,512,512]{1,2,0:T(8,128)(2,1)} %get-tuple-element.529) | copy-start | bytes 3145732 | tf_op jit(solution)/shard_map/while
  184.5 3.0 %copy-start.4 = (bf16[2,512,8,64]{1,3,2,0:T(8,128)(2,1)S(1)}, bf16[2,512,8,64]{1,3,2,0:T(8,128)(2,1)}, u32[]{:S(2)}) copy-start(bf16[2,512,8,64]{1,3,2,0:T(8,128)(2,1)} %get-tuple-element.353) | copy-start | bytes 3145732 | tf_op jit(solution)/shard_map/while/body/eval_jaxpr/cond
  193.2 4.9 %copy-start.1 = (bf16[2,512,512]{1,2,0:T(8,128)(2,1)S(1)}, bf16[2,512,512]{1,2,0:T(8,128)(2,1)}, u32[]{:S(2)}) copy-start(bf16[2,512,512]{1,2,0:T(8,128)(2,1)} %copy-done) | copy-start | bytes 3145732 | tf_op jit(solution)/shard_map/while
  193.2 3.0 %copy-start.2 = (bf16[2,512,8,64]{1,3,2,0:T(8,128)(2,1)S(1)}, bf16[2,512,8,64]{1,3,2,0:T(8,128)(2,1)}, u32[]{:S(2)}) copy-start(bf16[2,512,8,64]{1,3,2,0:T(8,128)(2,1)} %get-tuple-element.363) | copy-start | bytes 3145732 | tf_op jit(solution)/shard_map/while/body/eval_jaxpr/cond
  210.1 15.3 %copy-start = (bf16[2,512,512]{1,2,0:T(8,128)(2,1)}, bf16[2,512,512]{1,2,0:T(8,128)(2,1)S(1)}, u32[]{:S(2)}) copy-start(bf16[2,512,512]{1,2,0:T(8,128)(2,1)S(1)} %get-tuple-element.531) | copy-start | bytes 3145732 | tf_op jit(solution)/shard_map/while
  229.0 4.9 %copy-start.5 = (bf16[2,512,512]{1,2,0:T(8,128)(2,1)S(1)}, bf16[2,512,512]{1,2,0:T(8,128)(2,1)}, u32[]{:S(2)}) copy-start(bf16[2,512,512]{1,2,0:T(8,128)(2,1)} %get-tuple-element.527) | copy-start | bytes 3145732 | tf_op jit(solution)/shard_map/while
  229.0 3.0 %copy-start.6 = (bf16[2,512,8,64]{1,3,2,0:T(8,128)(2,1)S(1)}, bf16[2,512,8,64]{1,3,2,0:T(8,128)(2,1)}, u32[]{:S(2)}) copy-start(bf16[2,512,8,64]{1,3,2,0:T(8,128)(2,1)} %get-tuple-element.343) | copy-start | bytes 3145732 | tf_op jit(solution)/shard_map/while/body/eval_jaxpr/cond
  237.8 4.9 %copy-start.3 = (bf16[2,512,512]{1,2,0:T(8,128)(2,1)S(1)}, bf16[2,512,512]{1,2,0:T(8,128)(2,1)}, u32[]{:S(2)}) copy-start(bf16[2,512,512]{1,2,0:T(8,128)(2,1)} %get-tuple-element.529) | copy-start | bytes 3145732 | tf_op jit(solution)/shard_map/while
  237.8 3.0 %copy-start.4 = (bf16[2,512,8,64]{1,3,2,0:T(8,128)(2,1)S(1)}, bf16[2,512,8,64]{1,3,2,0:T(8,128)(2,1)}, u32[]{:S(2)}) copy-start(bf16[2,512,8,64]{1,3,2,0:T(8,128)(2,1)} %get-tuple-element.353) | copy-start | bytes 3145732 | tf_op jit(solution)/shard_map/while/body/eval_jaxpr/cond
  242.6 1.2 copy-start.1
